TPU v7x, 32 devices: a whole 2x2x4 slice. The times are simulated.
32 devices in a mesh: doc: 8 (over y, x, core), seq: 4 (over z).
Axes of the slice: x: 2, y: 2, z: 4, core: 2. Of those that a mesh axis runs over, the one named last changes fastest.
Arguments:
- inputs: bfloat16 [16, 1024, 768], P('doc', 'seq'), may hold values from -6 to 6
- attn_gain: float32 [768], replicated, may hold values from 0.5 to 1.5
- qkv_weight: bfloat16 [768, 2304], replicated, may hold values from -0.25 to 0.25
- attn_out_weight: bfloat16 [768, 768], replicated, may hold values from -2 to 2
- mlp_gain: float32 [768], replicated, may hold values from 0.5 to 1.5
- mlp_in_weight: bfloat16 [768, 2304], replicated, may hold values from -0.21875 to 0.21875
- mlp_out_weight: bfloat16 [1152, 768], replicated, may hold values from -0.1875 to 0.1875
- cotangent: bfloat16 [16, 1024, 768], P('doc', 'seq'), may hold values from -6 to 6
Outputs:
- output: bfloat16 [16, 1024, 768], P('doc', 'seq')
- input_grad: bfloat16 [16, 1024, 768], P('doc', 'seq')
- attn_gain_grad: float32 [768], replicated
- qkv_weight_grad: float32 [768, 2304], replicated
- attn_out_weight_grad: float32 [768, 768], replicated
- mlp_gain_grad: float32 [768], replicated
- mlp_in_weight_grad: float32 [768, 2304], replicated
- mlp_out_weight_grad: float32 [1152, 768], replicated
All inputs are finite; a program needn't handle non-finite values.
Results may differ from a plain program's by a relative error of at most 0.015.
Values may be sent and summed in bfloat16 or wider, within the bound.
A program may use at most 128 MiB of HBM per device.

v0:
```python
import jax
import jax.numpy as jnp
from jax import lax
from jax.sharding import PartitionSpec as P

HEAD_DIM = 64
ROPE_THETA = 160000.0
NORM_EPSILON = 1e-05


def norm_rows(values, scale_gain):
    row_mean = jnp.mean(values, axis=-1, keepdims=True)
    centered = values - row_mean
    variance = jnp.mean(centered * centered, axis=-1, keepdims=True)
    return centered * lax.rsqrt(variance + NORM_EPSILON) * scale_gain


def rotary_tables(positions, head_width):
    half_width = head_width // 2
    frequency = ROPE_THETA ** (-(jnp.arange(half_width, dtype=jnp.float32) * 2.0) / head_width)
    angles = positions.astype(jnp.float32)[:, None] * frequency[None, :]
    angles = jnp.concatenate([angles, angles], axis=-1)
    return (jnp.cos(angles)[:, None, :], jnp.sin(angles)[:, None, :])


def rotate(values, cosine_table, sine_table):
    half_width = values.shape[-1] // 2
    turned = jnp.concatenate([-values[..., half_width:], values[..., :half_width]], axis=-1)
    return values * cosine_table + turned * sine_table


def rotate_back(gradient, cosine_table, sine_table):
    half_width = gradient.shape[-1] // 2
    sined = gradient * sine_table
    turned = jnp.concatenate([sined[..., half_width:], -sined[..., :half_width]], axis=-1)
    return gradient * cosine_table + turned


def gelu_product(gate_up):
    half_width = gate_up.shape[-1] // 2
    return jax.nn.gelu(gate_up[..., :half_width], approximate=False) * gate_up[..., half_width:]


def split_heads(columns):
    return columns.reshape(columns.shape[0], columns.shape[1] // HEAD_DIM, HEAD_DIM)


def attend_forward(queries, key_rows, value_rows):
    length, features = queries.shape
    scores = (
        jnp.einsum(
            "qhd,khd->hqk",
            split_heads(queries),
            split_heads(key_rows),
            preferred_element_type=jnp.float32,
        )
        * 0.125
    )
    row_max = jnp.max(scores, axis=-1, keepdims=True)
    exp_scores = jnp.exp(scores - row_max)
    row_total = jnp.sum(exp_scores, axis=-1, keepdims=True)
    softmax_low = (exp_scores / row_total).astype(jnp.bfloat16)
    mixed_rows = jnp.einsum(
        "hqk,khd->qhd", softmax_low, split_heads(value_rows), preferred_element_type=jnp.float32
    )
    return (
        mixed_rows.reshape(length, features).astype(jnp.bfloat16),
        (row_max + jnp.log(row_total))[..., 0],
    )


def attend_backward(queries, key_rows, value_rows, grad_mixed, log_total, cosine_table, sine_table):
    length, features = queries.shape
    query_heads = split_heads(queries)
    key_heads = split_heads(key_rows)
    value_heads = split_heads(value_rows)
    grad_heads = split_heads(grad_mixed)
    scores = (
        jnp.einsum("qhd,khd->hqk", query_heads, key_heads, preferred_element_type=jnp.float32)
        * 0.125
    )
    softmax_out = jnp.exp(scores - log_total[..., None])
    grad_soft = jnp.einsum(
        "qhd,khd->hqk", grad_heads, value_heads, preferred_element_type=jnp.float32
    )
    row_inner = jnp.sum(softmax_out * grad_soft, axis=-1, keepdims=True)
    grad_scores = (softmax_out * (grad_soft - row_inner)).astype(jnp.bfloat16)
    grad_query = (
        jnp.einsum("hqk,khd->qhd", grad_scores, key_heads, preferred_element_type=jnp.float32)
        * 0.125
    )
    grad_key = (
        jnp.einsum("hqk,qhd->khd", grad_scores, query_heads, preferred_element_type=jnp.float32)
        * 0.125
    )
    grad_value = jnp.einsum(
        "hqk,qhd->khd",
        softmax_out.astype(jnp.bfloat16),
        grad_heads,
        preferred_element_type=jnp.float32,
    )
    grad_query = (
        rotate_back(grad_query, cosine_table, sine_table)
        .reshape(length, features)
        .astype(jnp.bfloat16)
    )
    grad_key = (
        rotate_back(grad_key, cosine_table, sine_table)
        .reshape(length, features)
        .astype(jnp.bfloat16)
    )
    return (grad_query, grad_key, grad_value.reshape(length, features).astype(jnp.bfloat16))


def per_device(
    inputs,
    attn_gain,
    qkv_weight,
    attn_out_weight,
    mlp_gain,
    mlp_in_weight,
    mlp_out_weight,
    cotangent,
):
    doc_count, row_count, features = inputs.shape
    token_count = doc_count * row_count
    length = row_count * lax.axis_size("seq")
    flat_in = inputs.reshape(token_count, features).astype(jnp.float32)
    normed = norm_rows(flat_in, attn_gain).astype(jnp.bfloat16)
    projected = jnp.dot(normed, qkv_weight, preferred_element_type=jnp.float32)
    projected = projected.reshape(doc_count, row_count, 3 * features)
    local_cos, local_sin = rotary_tables(
        lax.axis_index("seq") * row_count + jnp.arange(row_count, dtype=jnp.int32), HEAD_DIM
    )

    def turned_low(columns):
        shaped = columns.reshape(doc_count, row_count, features // HEAD_DIM, HEAD_DIM)
        return (
            rotate(shaped, local_cos, local_sin)
            .reshape(doc_count, row_count, features)
            .astype(jnp.bfloat16)
        )

    queries = turned_low(projected[..., :features])
    key_rows = turned_low(projected[..., features : 2 * features])
    value_rows = projected[..., 2 * features :].astype(jnp.bfloat16)
    head_queries, head_keys, head_values = (
        lax.all_to_all(queries, "seq", split_axis=2, concat_axis=1, tiled=True),
        lax.all_to_all(key_rows, "seq", split_axis=2, concat_axis=1, tiled=True),
        lax.all_to_all(value_rows, "seq", split_axis=2, concat_axis=1, tiled=True),
    )
    mixed_heads, log_total = lax.map(
        lambda bundle: attend_forward(*bundle), (head_queries, head_keys, head_values)
    )
    attended = lax.all_to_all(mixed_heads, "seq", split_axis=1, concat_axis=2, tiled=True).reshape(
        token_count, features
    )
    hidden_res = flat_in + jnp.dot(attended, attn_out_weight, preferred_element_type=jnp.float32)
    normed_two = norm_rows(hidden_res, mlp_gain).astype(jnp.bfloat16)
    gate_up = jnp.dot(normed_two, mlp_in_weight, preferred_element_type=jnp.float32)
    inner_act, inner_pull = jax.vjp(gelu_product, gate_up)
    inner_act = inner_act.astype(jnp.bfloat16)
    result = hidden_res + jnp.dot(inner_act, mlp_out_weight, preferred_element_type=jnp.float32)
    output = result.astype(jnp.bfloat16).reshape(doc_count, row_count, features)
    upstream = cotangent.reshape(token_count, features)
    grad_mlp_out = jnp.einsum("tf,td->fd", inner_act, upstream, preferred_element_type=jnp.float32)
    grad_inner = jnp.einsum(
        "td,fd->tf", upstream, mlp_out_weight, preferred_element_type=jnp.float32
    )
    grad_gate_up = inner_pull(grad_inner)[0].astype(jnp.bfloat16)
    grad_mlp_in = jnp.einsum(
        "td,tf->df", normed_two, grad_gate_up, preferred_element_type=jnp.float32
    )
    grad_normed_two = jnp.einsum(
        "tf,df->td", grad_gate_up, mlp_in_weight, preferred_element_type=jnp.float32
    )
    _, second_pull = jax.vjp(norm_rows, hidden_res, mlp_gain)
    grad_hidden, grad_mlp_gain = second_pull(grad_normed_two)
    grad_hidden = grad_hidden + upstream.astype(jnp.float32)
    grad_branch = grad_hidden.astype(jnp.bfloat16)
    grad_attn_out = jnp.einsum(
        "td,te->de", attended, grad_branch, preferred_element_type=jnp.float32
    )
    grad_attended = jnp.einsum(
        "te,de->td", grad_branch, attn_out_weight, preferred_element_type=jnp.float32
    )
    grad_attended = grad_attended.astype(jnp.bfloat16).reshape(doc_count, row_count, features)
    grad_mixed = lax.all_to_all(grad_attended, "seq", split_axis=2, concat_axis=1, tiled=True)
    full_cos, full_sin = rotary_tables(jnp.arange(length, dtype=jnp.int32), HEAD_DIM)
    grad_head_q, grad_head_k, grad_head_v = lax.map(
        lambda bundle: attend_backward(*bundle, full_cos, full_sin),
        (head_queries, head_keys, head_values, grad_mixed, log_total),
    )
    grad_tok_q, grad_tok_k, grad_tok_v = (
        lax.all_to_all(grad_head_q, "seq", split_axis=1, concat_axis=2, tiled=True),
        lax.all_to_all(grad_head_k, "seq", split_axis=1, concat_axis=2, tiled=True),
        lax.all_to_all(grad_head_v, "seq", split_axis=1, concat_axis=2, tiled=True),
    )
    grad_tok_q = grad_tok_q.reshape(token_count, features)
    grad_tok_k = grad_tok_k.reshape(token_count, features)
    grad_tok_v = grad_tok_v.reshape(token_count, features)
    grad_qkv = jnp.concatenate(
        [
            jnp.einsum("td,te->de", normed, grad_tok_q, preferred_element_type=jnp.float32),
            jnp.einsum("td,te->de", normed, grad_tok_k, preferred_element_type=jnp.float32),
            jnp.einsum("td,te->de", normed, grad_tok_v, preferred_element_type=jnp.float32),
        ],
        axis=1,
    )
    grad_normed = jnp.einsum(
        "te,de->td", grad_tok_q, qkv_weight[:, :features], preferred_element_type=jnp.float32
    )
    grad_normed = grad_normed + jnp.einsum(
        "te,de->td",
        grad_tok_k,
        qkv_weight[:, features : 2 * features],
        preferred_element_type=jnp.float32,
    )
    grad_normed = grad_normed + jnp.einsum(
        "te,de->td", grad_tok_v, qkv_weight[:, 2 * features :], preferred_element_type=jnp.float32
    )
    _, first_pull = jax.vjp(norm_rows, flat_in, attn_gain)
    grad_input, grad_attn_gain = first_pull(grad_normed)
    grad_input = (
        (grad_input + grad_hidden).astype(jnp.bfloat16).reshape(doc_count, row_count, features)
    )
    summed = lax.psum(
        (grad_attn_gain, grad_qkv, grad_attn_out, grad_mlp_gain, grad_mlp_in, grad_mlp_out),
        ("doc", "seq"),
    )
    return (output, grad_input, summed[0], summed[1], summed[2], summed[3], summed[4], summed[5])


def solution(mesh):
    placed = (P("doc", "seq", None), P(), P(), P(), P(), P(), P(), P("doc", "seq", None))
    return jax.shard_map(
        per_device,
        mesh=mesh,
        in_specs=placed,
        out_specs=(P("doc", "seq", None), P("doc", "seq", None), P(), P(), P(), P(), P(), P()),
        check_vma=False,
    )
```

profile of v0, /device:TPU:0, one launch (start us, length us, event | category | flops | bytes accessed | tf_op | source)
XLA Modules:
  0.0 743.3 jit_solution(14533819958164597936)
XLA Ops:
  23.3 6.3 all-to-all-start
  59.2 5.0 add_convert_fusion.3
  67.2 5.1 all-to-all-start.1
  75.3 16.6 %all-to-all-done.1 = bf16[2,256,768]{1,0,2:T(2,128)(2,1)} async-done(((bf16[2,256,768]{1,0,2:T(2,128)(2,1)}), bf16[2,256,768]{1,0,2:T(2,128)(2,1)}, u32[]{:S(2)}, u32[]{:S(2)}) %all-to-all-start.1) | async-done | bytes 786464 | tf_op jit(solution)/shard_map/all_to_all | solution.py:148
  91.9 4.4 all-to-all-start.2
  100.8 15.2 %all-to-all-done.2 = bf16[2,256,768]{1,0,2:T(2,128)(2,1)} async-done(((bf16[2,256,768]{1,0,2:T(2,128)(2,1)}), bf16[2,256,768]{1,0,2:T(2,128)(2,1)}, u32[]{:S(2)}, u32[]{:S(2)}) %all-to-all-start.2) | async-done | bytes 786464 | tf_op jit(solution)/shard_map/all_to_all | solution.py:149
  119.2 19.5 %while.26 = (s32[]{:T(128)}, bf16[2,1024,192]{1,2,0:T(8,128)(2,1)}, f32[2,3,1024]{2,1,0:T(4,128)}, bf16[2,1024,192]{1,2,0:T(8,128)(2,1)}, bf16[2,1024,192]{1,2,0...) while((s32[]{:T(128)}, bf16[2,1024,192]{1,2,0:T(8,128)(2,1)}, f32[2,3,1024]{2,1,0:T(4,128)}, ...), condition=%wide.region_5.6_spmd, body=%wide.region_2.5_spmd.sunk | while | flops 833811456 | bytes 48861340 | solution.py:152
  142.3 29.5 %all_to_all.132 = bf16[2,1024,192]{2,0,1:T(2,128)(2,1)} all-to-all(bf16[2,1024,192]{2,0,1:T(2,128)(2,1)} %copy.86), channel_id=1, replica_groups=mesh['doc'=8,'seq'=4] {'seq'}, dimensions={1} | all-to-all | bytes 1572864 | tf_op jit(solution)/shard_map/all_to_all | solution.py:155
  171.8 5.9 copy.87
  184.3 5.6 fusion.39
  205.8 17.4 %all-to-all-done.4 = bf16[2,256,768]{1,0,2:T(2,128)(2,1)S(1)} async-done(((bf16[2,256,768]{1,0,2:T(2,128)(2,1)}), bf16[2,256,768]{1,0,2:T(2,128)(2,1)S(1)}, u32[]{:S(2)}, u32[]{:S(2)}) %all-to-all-start.4) | async-done | bytes 786464 | tf_op jit(solution)/shard_map/all_to_all | solution.py:188
  227.2 60.3 %while.27 = (s32[]{:T(128)}, bf16[2,1024,192]{1,2,0:T(8,128)(2,1)}, bf16[2,1024,192]{1,2,0:T(8,128)(2,1)}, bf16[2,1024,192]{1,2,0:T(8,128)(2,1)}, bf16[2,1024,19...) while((s32[]{:T(128)}, bf16[2,1024,192]{1,2,0:T(8,128)(2,1)}, ...), condition=%wide.region_12.13_spmd, body=%wide.region_10.12_spmd.sunk | while | flops 2053501952 | bytes 154489168 | solution.py:190
  242.3 5.3 multiply_convert_fusion.6
  272.5 5.3 multiply_convert_fusion.6
  296.8 23.1 %all-to-all-done.7 = bf16[2,1024,192]{2,0,1:T(2,128)(2,1)S(1)} async-done(((bf16[2,1024,192]{2,0,1:T(2,128)(2,1)}), bf16[2,1024,192]{2,0,1:T(2,128)(2,1)S(1)}, u32[]{:S(2)}, u32[]{:S(2)}) %all-to-all-start.7) | async-done | bytes 786464 | tf_op jit(solution)/shard_map/all_to_all | solution.py:197
  325.5 23.1 %all-to-all-done.5 = bf16[2,1024,192]{2,0,1:T(2,128)(2,1)S(1)} async-done(((bf16[2,1024,192]{2,0,1:T(2,128)(2,1)}), bf16[2,1024,192]{2,0,1:T(2,128)(2,1)S(1)}, u32[]{:S(2)}, u32[]{:S(2)}) %all-to-all-start.5) | async-done | bytes 786464 | tf_op jit(solution)/shard_map/all_to_all | solution.py:195
  360.9 5.2 fusion.40
  366.1 4.7 copy.96
  371.9 5.7 copy.92
  379.8 5.7 copy.94
  403.7 43.1 %all-reduce.2 = (f32[768]{0:T(1024)}, f32[768]{0:T(1024)}) all-reduce(f32[768]{0:T(1024)S(1)} %get-tuple-element.139, f32[768]{0:T(1024)S(1)} %copy-done.49), channel_id=1, replica_groups=mesh['doc'=8,'seq'=4] {'doc','seq'}, use_global_device_ids=true, to_apply=%region_16.17 | all-reduce | flops 1536 | bytes 12288 | tf_op jit(solution)/shard_map/psum | solution.py:227
  449.8 268.4 %all-reduce.6.cloned.1.call-done = (f32[768,2304]{0,1:T(8,128)}, f32[768,768]{1,0:T(8,128)}, f32[768,2304]{1,0:T(8,128)}, f32[1152,768]{1,0:T(8,128)}) async-done(((f32[768,2304]{0,1:T(8,128)}, f32[768,768]{1,0:T(8,128)}, f32[768,2304]{1,0:T(8,128)}, f32[1152,768]{1,0:T(8,128)}), (f32[768,2304]{0,1:T(8,128)}, f32[768,768]{1,0:T(8,128)}, f32[768,2304]{1,0:T(8,128)}, ...) | async-done | bytes 20054032 | tf_op jit(solution)/shard_map/psum | solution.py:227
  718.3 8.1 %copy.97 = f32[768,2304]{1,0:T(8,128)} copy(f32[768,2304]{0,1:T(8,128)} %get-tuple-element.177) | data formatting | bytes 14155776
  727.8 6.6 copy.145
  (260 shorter events, 212.7 us)
Async XLA Ops:
  7.2 174.9 %copy-start = (bf16[768,2304]{1,0:T(8,128)(2,1)S(1)}, bf16[768,2304]{1,0:T(8,128)(2,1)}, u32[]{:S(2)}) copy-start(bf16[768,2304]{1,0:T(8,128)(2,1)} %param.17) | copy-start | bytes 10616836
  23.3 43.9 %all-to-all-start = ((bf16[2,256,768]{1,0,2:T(2,128)(2,1)}), bf16[2,256,768]{1,0,2:T(2,128)(2,1)}, u32[]{:S(2)}, u32[]{:S(2)}) async-start(bf16[2,256,768]{1,0,2:T(2,128)(2,1)} %copy.71), calls=%async_computation | async-start | bytes 1572864 | tf_op jit(solution)/shard_map/all_to_all | solution.py:150
  33.5 8.8 %copy-start.50 = (f32[32]{0:T(128)}, f32[32]{0:T(128)S(1)}, u32[]{:S(2)}) copy-start(f32[32]{0:T(128)S(1)} %multiply_power_fusion) | copy-start | bytes 388
  67.2 24.7 %all-to-all-start.1 = ((bf16[2,256,768]{1,0,2:T(2,128)(2,1)}), bf16[2,256,768]{1,0,2:T(2,128)(2,1)}, u32[]{:S(2)}, u32[]{:S(2)}) async-start(bf16[2,256,768]{1,0,2:T(2,128)(2,1)} %copy.78), calls=%async_computation.1 | async-start | bytes 1572864 | tf_op jit(solution)/shard_map/all_to_all | solution.py:148
  91.9 24.0 %all-to-all-start.2 = ((bf16[2,256,768]{1,0,2:T(2,128)(2,1)}), bf16[2,256,768]{1,0,2:T(2,128)(2,1)}, u32[]{:S(2)}, u32[]{:S(2)}) async-start(bf16[2,256,768]{1,0,2:T(2,128)(2,1)} %copy.83), calls=%async_computation.2 | async-start | bytes 1572864 | tf_op jit(solution)/shard_map/all_to_all | solution.py:149
  181.7 13.2 %copy-start.6 = (f32[512,768]{1,0:T(8,128)}, f32[512,768]{1,0:T(8,128)S(1)}, u32[]{:S(2)}) copy-start(f32[512,768]{1,0:T(8,128)S(1)} %get-tuple-element.225) | copy-start | bytes 4718596
  181.8 13.2 %copy-start.41 = (f32[512]{0:T(512)}, f32[512]{0:T(512)S(1)}, u32[]{:S(2)}) copy-start(f32[512]{0:T(512)S(1)} %broadcast_multiply_fusion.3) | copy-start | bytes 6148
  182.1 12.8 %copy-start.43 = (f32[512]{0:T(512)}, f32[512]{0:T(512)S(1)}, u32[]{:S(2)}) copy-start(f32[512]{0:T(512)S(1)} %fusion.46) | copy-start | bytes 6148
  198.7 5.3 copy-start.51
  200.5 22.6 %all-to-all-start.4 = ((bf16[2,256,768]{1,0,2:T(2,128)(2,1)}), bf16[2,256,768]{1,0,2:T(2,128)(2,1)S(1)}, u32[]{:S(2)}, u32[]{:S(2)}) async-start(bf16[2,256,768]{1,0,2:T(2,128)(2,1)} %copy.88), calls=%async_computation.4 | async-start | bytes 1572864 | tf_op jit(solution)/shard_map/all_to_all | solution.py:188
  247.6 4.6 copy-start.2
  287.5 7.2 copy-start.22
  291.2 28.7 %all-to-all-start.7 = ((bf16[2,1024,192]{2,0,1:T(2,128)(2,1)}), bf16[2,1024,192]{2,0,1:T(2,128)(2,1)S(1)}, u32[]{:S(2)}, u32[]{:S(2)}) async-start(bf16[2,1024,192]{2,0,1:T(2,128)(2,1)} %copy.95), calls=%async_computation.7 | async-start | bytes 2097152 | tf_op jit(solution)/shard_map/all_to_all | solution.py:197
  294.7 28.7 %copy-start.25 = (bf16[2,1024,192]{1,2,0:T(8,128)(2,1)S(1)}, bf16[2,1024,192]{1,2,0:T(8,128)(2,1)}, u32[]{:S(2)}) copy-start(bf16[2,1024,192]{1,2,0:T(8,128)(2,1)} %get-tuple-element.103) | copy-start | bytes 2359300
  319.9 28.7 %copy-start.17 = (bf16[2,1024,192]{2,0,1:T(2,128)(2,1)}, bf16[2,1024,192]{2,0,1:T(2,128)(2,1)S(1)}, u32[]{:S(2)}) copy-start(bf16[2,1024,192]{2,0,1:T(2,128)(2,1)S(1)} %all-to-all-done.7) | copy-start | bytes 2359300
  319.9 28.7 %all-to-all-start.5 = ((bf16[2,1024,192]{2,0,1:T(2,128)(2,1)}), bf16[2,1024,192]{2,0,1:T(2,128)(2,1)S(1)}, u32[]{:S(2)}, u32[]{:S(2)}) async-start(bf16[2,1024,192]{2,0,1:T(2,128)(2,1)} %copy.91), calls=%async_computation.5 | async-start | bytes 2097152 | tf_op jit(solution)/shard_map/all_to_all | solution.py:195
  348.6 8.1 %copy-start.18 = (bf16[2,1024,192]{2,0,1:T(2,128)(2,1)}, bf16[2,1024,192]{2,0,1:T(2,128)(2,1)S(1)}, u32[]{:S(2)}) copy-start(bf16[2,1024,192]{2,0,1:T(2,128)(2,1)S(1)} %all-to-all-done.5) | copy-start | bytes 2359300
  348.6 31.2 %all-to-all-start.6 = ((bf16[2,1024,192]{2,0,1:T(2,128)(2,1)}), bf16[2,1024,192]{2,0,1:T(2,128)(2,1)}, u32[]{:S(2)}, u32[]{:S(2)}) async-start(bf16[2,1024,192]{2,0,1:T(2,128)(2,1)} %copy.93), calls=%async_computation.6 | async-start | bytes 2097152 | tf_op jit(solution)/shard_map/all_to_all | solution.py:196
  352.9 365.4 %all-reduce.6.cloned.1.call-start = ((), (), s32[]{:S(2)}) async-start(), calls=%async_computation.8 | async-start | bytes 40108032 | tf_op jit(solution)/shard_map/psum | solution.py:227
  377.6 9.3 %copy-start.9 = (bf16[2,256,768]{2,1,0:T(8,128)(2,1)S(1)}, bf16[2,256,768]{2,1,0:T(8,128)(2,1)}, u32[]{:S(2)}) copy-start(bf16[2,256,768]{2,1,0:T(8,128)(2,1)} %copy-done.8) | copy-start | bytes 2359300
  402.9 44.0 %copy-start.46 = (f32[512]{0:T(512)S(1)}, f32[512]{0:T(512)}, u32[]{:S(2)}) copy-start(f32[512]{0:T(512)} %copy-done.45) | copy-start | bytes 6148
  718.3 8.1 %copy-start.34 = (f32[768,768]{1,0:T(8,128)S(1)}, f32[768,768]{1,0:T(8,128)}, u32[]{:S(2)}) copy-start(f32[768,768]{1,0:T(8,128)} %get-tuple-element.433) | copy-start | bytes 7077892
  727.8 6.6 copy-start.19
  727.8 8.4 %copy-start.1 = (bf16[768,2304]{1,0:T(8,128)(2,1)S(1)}, bf16[768,2304]{1,0:T(8,128)(2,1)}, u32[]{:S(2)}) copy-start(bf16[768,2304]{1,0:T(8,128)(2,1)} %param.17) | copy-start | bytes 10616836
  (46 other events, 101.6 us)
Sparse Core Ops, SparseCore 0:
  394.3 323.9 all-reduce.5
where the time goes:
time: 752 us; the launch traced here: 743 us
  waiting for transfers between devices  364 us (48%)
  local copies, waits for them, and re-layouts  133 us (18%)
  matrix products  77.8 us (10%)
  blocking collectives  72.7 us (10%)
  other arithmetic  49.8 us (7%)
  starting transfers between devices  30.8 us (4%)
  between operations  14.9 us (2%)
    psum x1, waiting for transfers between devices, per_device(): lax.psum((grad_attn_gain, grad_qkv, grad_attn_out, grad_mlp_gain, grad_ml...  268 us
    psum x1, blocking collectives, per_device(): lax.psum((grad_attn_gain, grad_qkv, grad_attn_out, grad_mlp_gain, grad_ml...  43.1 us
    unnamed x102, local copies, waits for them, and re-layouts  30.9 us
    all_to_all x1, blocking collectives, per_device(): lax.all_to_all(mixed_heads, 'seq', split_axis=1, concat_axis=2, tiled=True)  29.5 us
    all_to_all x1, waiting for transfers between devices, per_device(): lax.all_to_all(grad_head_v, 'seq', split_axis=1, concat_axis=2, tiled=True)  23.1 us
    all_to_all x1, waiting for transfers between devices, per_device(): lax.all_to_all(grad_head_q, 'seq', split_axis=1, concat_axis=2, tiled=True)  23.1 us
    all_to_all x1, waiting for transfers between devices, per_device(): lax.all_to_all(grad_attended, 'seq', split_axis=2, concat_axis=1, tiled=T...  17.4 us
    all_to_all x1, waiting for transfers between devices, per_device(): lax.all_to_all(queries, 'seq', split_axis=2, concat_axis=1, tiled=True)  16.6 us
  transfers between devices with their start and end apart: 8, of which 6 were waited for; matrix products, arithmetic and copies ran while one was open for 12% of the time, Pallas kernels for 0%

commit v1 on v0

--- a/solution.py
+++ b/solution.py
@@ -6,6 +6,29 @@
 HEAD_DIM = 64
 ROPE_THETA = 160000.0
 NORM_EPSILON = 1e-05
+
+
+def in_blocks(x, dim, length):
+    lengths = x.shape
+    pieces = x.reshape(*lengths[:dim], length, lengths[dim] // length, *lengths[dim + 1 :])
+    return jnp.moveaxis(pieces, dim, 0)
+
+
+def laid_out(blocks, dim):
+    shape = list(blocks.shape[1:])
+    shape[dim] *= blocks.shape[0]
+    return jnp.moveaxis(blocks, 0, dim).reshape(shape)
+
+
+def swapped_with_each(shard, axis, split_dim, concat_dim):
+    size, index = (lax.axis_size(axis), lax.axis_index(axis))
+    blocks = in_blocks(shard, split_dim, size)
+    done = [blocks[index]]
+    for lap in range(1, size):
+        sent = blocks[index ^ lap]
+        done.append(lax.ppermute(sent, axis, [(i, i ^ lap) for i in range(size)]))
+    blocks = jnp.stack(done)[index ^ jnp.arange(size)]
+    return laid_out(blocks, concat_dim)
 
 
 def norm_rows(values, scale_gain):
@@ -145,7 +168,7 @@
     key_rows = turned_low(projected[..., features : 2 * features])
     value_rows = projected[..., 2 * features :].astype(jnp.bfloat16)
     head_queries, head_keys, head_values = (
-        lax.all_to_all(queries, "seq", split_axis=2, concat_axis=1, tiled=True),
+        swapped_with_each(queries, "seq", 2, 1),
         lax.all_to_all(key_rows, "seq", split_axis=2, concat_axis=1, tiled=True),
         lax.all_to_all(value_rows, "seq", split_axis=2, concat_axis=1, tiled=True),
     )

time: 752 us -> 754 us (level)
    ppermute x0 -> x3, waiting for transfers between devices: none -> 27.7 us  [swapped_with_each(): done.append(lax.ppermute(sent, axis, [(i, i ^ lap) for i in range(size)]))]
    all_to_all x1 -> x0, waiting for transfers between devices: 16.6 us -> none  [per_device(): lax.all_to_all(queries, 'seq', split_axis=2, concat_axis=1, tiled=True)]
    all_to_all x1, waiting for transfers between devices: 15.2 us -> 0.01 us  [per_device(): lax.all_to_all(key_rows, 'seq', split_axis=2, concat_axis=1, tiled=True)]
  transfers between devices with their start and end apart: 8 -> 10, of which waited for: 6 -> 6; matrix products, arithmetic and copies ran while one was open for 12% -> 12% of each run, Pallas kernels for 0% -> 0%
where the time goes in v1:
time: 754 us; the launch traced here: 745 us
  waiting for transfers between devices  360 us (48%)
  local copies, waits for them, and re-layouts  137 us (18%)
  matrix products  77.7 us (10%)
  blocking collectives  72.7 us (10%)
  other arithmetic  52 us (7%)
  starting transfers between devices  31 us (4%)
  between operations  14.9 us (2%)
    psum x1, waiting for transfers between devices, per_device(): lax.psum((grad_attn_gain, grad_qkv, grad_attn_out, grad_mlp_gain, grad_ml...  268 us
    psum x1, blocking collectives, per_device(): lax.psum((grad_attn_gain, grad_qkv, grad_attn_out, grad_mlp_gain, grad_ml...  43.2 us
    unnamed x102, local copies, waits for them, and re-layouts  30.9 us
    all_to_all x1, blocking collectives, per_device(): lax.all_to_all(mixed_heads, 'seq', split_axis=1, concat_axis=2, tiled=True)  29.5 us
    ppermute x3, waiting for transfers between devices, swapped_with_each(): done.append(lax.ppermute(sent, axis, [(i, i ^ lap) for i in range(size)]))  27.7 us
    all_to_all x1, waiting for transfers between devices, per_device(): lax.all_to_all(grad_head_v, 'seq', split_axis=1, concat_axis=2, tiled=True)  23.1 us
    all_to_all x1, waiting for transfers between devices, per_device(): lax.all_to_all(grad_head_q, 'seq', split_axis=1, concat_axis=2, tiled=True)  23.1 us
    all_to_all x1, waiting for transfers between devices, per_device(): lax.all_to_all(grad_attended, 'seq', split_axis=2, concat_axis=1, tiled=T...  17.4 us
  transfers between devices with their start and end apart: 10, of which 6 were waited for; matrix products, arithmetic and copies ran while one was open for 12% of the time, Pallas kernels for 0%

profile of v1, /device:TPU:0, one launch (start us, length us, event | category | flops | bytes accessed | tf_op | source)
XLA Modules:
  0.0 745.4 jit_solution(16190331889369114551)
XLA Ops:
  12.8 4.3 fusion.13
  23.3 6.3 all-to-all-start
  59.2 5.0 add_convert_fusion.3
  67.2 5.3 all-to-all-start.1
  81.3 13.7 %collective-permute-done.2 = bf16[2,256,192]{1,2,0:T(8,128)(2,1)} collective-permute-done((bf16[2,256,192]{1,2,0:T(8,128)(2,1)}, bf16[2,256,192]{1,2,0:T(8,128)(2,1)}, u32[]{:S(2)}, u32[]{:S(2)}) %collective-permute-start.2) | collective-permute-done | bytes 196640 | tf_op jit(solution)/shard_map/ppermute | solution.py:29
  95.0 13.9 %collective-permute-done.1 = bf16[2,256,192]{1,2,0:T(8,128)(2,1)} collective-permute-done((bf16[2,256,192]{1,2,0:T(8,128)(2,1)}, bf16[2,256,192]{1,2,0:T(8,128)(2,1)}, u32[]{:S(2)}, u32[]{:S(2)}) %collective-permute-start.1) | collective-permute-done | bytes 196640 | tf_op jit(solution)/shard_map/ppermute | solution.py:29
  121.3 19.5 %while.26 = (s32[]{:T(128)}, bf16[2,1024,192]{1,2,0:T(8,128)(2,1)}, f32[2,3,1024]{2,1,0:T(4,128)}, bf16[2,1024,192]{1,2,0:T(8,128)(2,1)}, bf16[2,1024,192]{1,2,0...) while((s32[]{:T(128)}, bf16[2,1024,192]{1,2,0:T(8,128)(2,1)}, f32[2,3,1024]{2,1,0:T(4,128)}, ...), condition=%wide.region_5.6_spmd, body=%wide.region_2.5_spmd.sunk | while | flops 833811456 | bytes 48861340 | solution.py:175
  144.4 29.5 %all_to_all.114 = bf16[2,1024,192]{2,0,1:T(2,128)(2,1)} all-to-all(bf16[2,1024,192]{2,0,1:T(2,128)(2,1)} %copy.84), channel_id=1, replica_groups=mesh['doc'=8,'seq'=4] {'seq'}, dimensions={1} | all-to-all | bytes 1572864 | tf_op jit(solution)/shard_map/all_to_all | solution.py:178
  174.0 5.9 copy.85
  186.4 5.6 fusion.39
  207.9 17.4 %all-to-all-done.3 = bf16[2,256,768]{1,0,2:T(2,128)(2,1)S(1)} async-done(((bf16[2,256,768]{1,0,2:T(2,128)(2,1)}), bf16[2,256,768]{1,0,2:T(2,128)(2,1)S(1)}, u32[]{:S(2)}, u32[]{:S(2)}) %all-to-all-start.3) | async-done | bytes 786464 | tf_op jit(solution)/shard_map/all_to_all | solution.py:211
  229.3 60.3 %while.27 = (s32[]{:T(128)}, bf16[2,1024,192]{1,2,0:T(8,128)(2,1)}, bf16[2,1024,192]{1,2,0:T(8,128)(2,1)}, bf16[2,1024,192]{1,2,0:T(8,128)(2,1)}, bf16[2,1024,19...) while((s32[]{:T(128)}, bf16[2,1024,192]{1,2,0:T(8,128)(2,1)}, ...), condition=%wide.region_12.13_spmd, body=%wide.region_10.12_spmd.sunk | while | flops 2053501952 | bytes 154489168 | solution.py:213
  244.5 5.3 multiply_convert_fusion.6
  274.7 5.3 multiply_convert_fusion.6
  298.9 23.1 %all-to-all-done.6 = bf16[2,1024,192]{2,0,1:T(2,128)(2,1)S(1)} async-done(((bf16[2,1024,192]{2,0,1:T(2,128)(2,1)}), bf16[2,1024,192]{2,0,1:T(2,128)(2,1)S(1)}, u32[]{:S(2)}, u32[]{:S(2)}) %all-to-all-start.6) | async-done | bytes 786464 | tf_op jit(solution)/shard_map/all_to_all | solution.py:220
  327.6 23.1 %all-to-all-done.4 = bf16[2,1024,192]{2,0,1:T(2,128)(2,1)S(1)} async-done(((bf16[2,1024,192]{2,0,1:T(2,128)(2,1)}), bf16[2,1024,192]{2,0,1:T(2,128)(2,1)S(1)}, u32[]{:S(2)}, u32[]{:S(2)}) %all-to-all-start.4) | async-done | bytes 786464 | tf_op jit(solution)/shard_map/all_to_all | solution.py:218
  363.1 5.2 fusion.40
  368.2 4.7 copy.94
  374.0 5.7 copy.90
  382.0 5.7 copy.92
  405.8 43.2 %all-reduce.2 = (f32[768]{0:T(1024)}, f32[768]{0:T(1024)}) all-reduce(f32[768]{0:T(1024)S(1)} %get-tuple-element.139, f32[768]{0:T(1024)S(1)} %copy-done.49), channel_id=1, replica_groups=mesh['doc'=8,'seq'=4] {'doc','seq'}, use_global_device_ids=true, to_apply=%region_16.17 | all-reduce | flops 1536 | bytes 12288 | tf_op jit(solution)/shard_map/psum | solution.py:250
  452.0 268.5 %all-reduce.6.cloned.1.call-done = (f32[768,2304]{0,1:T(8,128)}, f32[768,768]{1,0:T(8,128)}, f32[768,2304]{1,0:T(8,128)}, f32[1152,768]{1,0:T(8,128)}) async-done(((f32[768,2304]{0,1:T(8,128)}, f32[768,768]{1,0:T(8,128)}, f32[768,2304]{1,0:T(8,128)}, f32[1152,768]{1,0:T(8,128)}), (f32[768,2304]{0,1:T(8,128)}, f32[768,768]{1,0:T(8,128)}, f32[768,2304]{1,0:T(8,128)}, ...) | async-done | bytes 20054032 | tf_op jit(solution)/shard_map/psum | solution.py:250
  720.5 8.1 %copy.95 = f32[768,2304]{1,0:T(8,128)} copy(f32[768,2304]{0,1:T(8,128)} %get-tuple-element.177) | data formatting | bytes 14155776
  730.0 6.6 copy.143
  (268 shorter events, 218.8 us)
Async XLA Ops:
  7.2 177.1 %copy-start = (bf16[768,2304]{1,0:T(8,128)(2,1)S(1)}, bf16[768,2304]{1,0:T(8,128)(2,1)}, u32[]{:S(2)}) copy-start(bf16[768,2304]{1,0:T(8,128)(2,1)} %param.17) | copy-start | bytes 10616836
  23.3 43.9 %all-to-all-start = ((bf16[2,256,768]{1,0,2:T(2,128)(2,1)}), bf16[2,256,768]{1,0,2:T(2,128)(2,1)}, u32[]{:S(2)}, u32[]{:S(2)}) async-start(bf16[2,256,768]{1,0,2:T(2,128)(2,1)} %copy.70), calls=%async_computation | async-start | bytes 1572864 | tf_op jit(solution)/shard_map/all_to_all | solution.py:173
  33.5 8.8 %copy-start.50 = (f32[32]{0:T(128)}, f32[32]{0:T(128)S(1)}, u32[]{:S(2)}) copy-start(f32[32]{0:T(128)S(1)} %multiply_power_fusion) | copy-start | bytes 388
  67.2 50.9 %all-to-all-start.1 = ((bf16[2,256,768]{1,0,2:T(2,128)(2,1)}), bf16[2,256,768]{1,0,2:T(2,128)(2,1)}, u32[]{:S(2)}, u32[]{:S(2)}) async-start(bf16[2,256,768]{1,0,2:T(2,128)(2,1)} %copy.81), calls=%async_computation.1 | async-start | bytes 1572864 | tf_op jit(solution)/shard_map/all_to_all | solution.py:172
  76.9 18.2 %collective-permute-start.2 = (bf16[2,256,192]{1,2,0:T(8,128)(2,1)}, bf16[2,256,192]{1,2,0:T(8,128)(2,1)}, u32[]{:S(2)}, u32[]{:S(2)}) collective-permute-start(bf16[2,256,192]{1,2,0:T(8,128)(2,1)} %get-tuple-element.215), channel_id=1, source_target_pairs={{0,3},{1,2},{2,1},{3,0},{4,7},{5,6},{6,5},{7,4},{8,11},{9,10},{10,... | collective-permute-start | bytes 589832 | tf_op jit(solution)/shard_map/ppermute | solution.py:29
  80.7 28.3 %collective-permute-start.1 = (bf16[2,256,192]{1,2,0:T(8,128)(2,1)}, bf16[2,256,192]{1,2,0:T(8,128)(2,1)}, u32[]{:S(2)}, u32[]{:S(2)}) collective-permute-start(bf16[2,256,192]{1,2,0:T(8,128)(2,1)} %get-tuple-element.216), channel_id=1, source_target_pairs={{0,2},{1,3},{2,0},{3,1},{4,6},{5,7},{6,4},{7,5},{8,10},{9,11},{10,... | collective-permute-start | bytes 589832 | tf_op jit(solution)/shard_map/ppermute | solution.py:29
  80.7 28.3 %collective-permute-start = (bf16[2,256,192]{1,2,0:T(8,128)(2,1)}, bf16[2,256,192]{1,2,0:T(8,128)(2,1)}, u32[]{:S(2)}, u32[]{:S(2)}) collective-permute-start(bf16[2,256,192]{1,2,0:T(8,128)(2,1)} %get-tuple-element.217), channel_id=1, source_target_pairs={{0,1},{1,0},{2,3},{3,2},{4,5},{5,4},{6,7},{7,6},{8,9},{9,8},{10,11... | collective-permute-start | bytes 589832 | tf_op jit(solution)/shard_map/ppermute | solution.py:29
  183.9 13.2 %copy-start.6 = (f32[512,768]{1,0:T(8,128)}, f32[512,768]{1,0:T(8,128)S(1)}, u32[]{:S(2)}) copy-start(f32[512,768]{1,0:T(8,128)S(1)} %get-tuple-element.229) | copy-start | bytes 4718596
  183.9 13.2 %copy-start.41 = (f32[512]{0:T(512)}, f32[512]{0:T(512)S(1)}, u32[]{:S(2)}) copy-start(f32[512]{0:T(512)S(1)} %broadcast_multiply_fusion.3) | copy-start | bytes 6148
  184.3 12.8 %copy-start.43 = (f32[512]{0:T(512)}, f32[512]{0:T(512)S(1)}, u32[]{:S(2)}) copy-start(f32[512]{0:T(512)S(1)} %fusion.46) | copy-start | bytes 6148
  202.6 22.6 %all-to-all-start.3 = ((bf16[2,256,768]{1,0,2:T(2,128)(2,1)}), bf16[2,256,768]{1,0,2:T(2,128)(2,1)S(1)}, u32[]{:S(2)}, u32[]{:S(2)}) async-start(bf16[2,256,768]{1,0,2:T(2,128)(2,1)} %copy.86), calls=%async_computation.3 | async-start | bytes 1572864 | tf_op jit(solution)/shard_map/all_to_all | solution.py:211
  289.6 7.2 copy-start.22
  293.3 28.7 %all-to-all-start.6 = ((bf16[2,1024,192]{2,0,1:T(2,128)(2,1)}), bf16[2,1024,192]{2,0,1:T(2,128)(2,1)S(1)}, u32[]{:S(2)}, u32[]{:S(2)}) async-start(bf16[2,1024,192]{2,0,1:T(2,128)(2,1)} %copy.93), calls=%async_computation.6 | async-start | bytes 2097152 | tf_op jit(solution)/shard_map/all_to_all | solution.py:220
  296.9 28.7 %copy-start.25 = (bf16[2,1024,192]{1,2,0:T(8,128)(2,1)S(1)}, bf16[2,1024,192]{1,2,0:T(8,128)(2,1)}, u32[]{:S(2)}) copy-start(bf16[2,1024,192]{1,2,0:T(8,128)(2,1)} %get-tuple-element.103) | copy-start | bytes 2359300
  322.0 28.7 %copy-start.17 = (bf16[2,1024,192]{2,0,1:T(2,128)(2,1)}, bf16[2,1024,192]{2,0,1:T(2,128)(2,1)S(1)}, u32[]{:S(2)}) copy-start(bf16[2,1024,192]{2,0,1:T(2,128)(2,1)S(1)} %all-to-all-done.6) | copy-start | bytes 2359300
  322.0 28.7 %all-to-all-start.4 = ((bf16[2,1024,192]{2,0,1:T(2,128)(2,1)}), bf16[2,1024,192]{2,0,1:T(2,128)(2,1)S(1)}, u32[]{:S(2)}, u32[]{:S(2)}) async-start(bf16[2,1024,192]{2,0,1:T(2,128)(2,1)} %copy.89), calls=%async_computation.4 | async-start | bytes 2097152 | tf_op jit(solution)/shard_map/all_to_all | solution.py:218
  350.7 8.2 %copy-start.18 = (bf16[2,1024,192]{2,0,1:T(2,128)(2,1)}, bf16[2,1024,192]{2,0,1:T(2,128)(2,1)S(1)}, u32[]{:S(2)}) copy-start(bf16[2,1024,192]{2,0,1:T(2,128)(2,1)S(1)} %all-to-all-done.4) | copy-start | bytes 2359300
  350.7 31.2 %all-to-all-start.5 = ((bf16[2,1024,192]{2,0,1:T(2,128)(2,1)}), bf16[2,1024,192]{2,0,1:T(2,128)(2,1)}, u32[]{:S(2)}, u32[]{:S(2)}) async-start(bf16[2,1024,192]{2,0,1:T(2,128)(2,1)} %copy.91), calls=%async_computation.5 | async-start | bytes 2097152 | tf_op jit(solution)/shard_map/all_to_all | solution.py:219
  355.0 365.4 %all-reduce.6.cloned.1.call-start = ((), (), s32[]{:S(2)}) async-start(), calls=%async_computation.7 | async-start | bytes 40108032 | tf_op jit(solution)/shard_map/psum | solution.py:250
  379.7 9.3 %copy-start.9 = (bf16[2,256,768]{2,1,0:T(8,128)(2,1)S(1)}, bf16[2,256,768]{2,1,0:T(8,128)(2,1)}, u32[]{:S(2)}) copy-start(bf16[2,256,768]{2,1,0:T(8,128)(2,1)} %copy-done.8) | copy-start | bytes 2359300
  405.0 44.0 %copy-start.46 = (f32[512]{0:T(512)S(1)}, f32[512]{0:T(512)}, u32[]{:S(2)}) copy-start(f32[512]{0:T(512)} %copy-done.45) | copy-start | bytes 6148
  720.5 8.1 %copy-start.34 = (f32[768,768]{1,0:T(8,128)S(1)}, f32[768,768]{1,0:T(8,128)}, u32[]{:S(2)}) copy-start(f32[768,768]{1,0:T(8,128)} %get-tuple-element.437) | copy-start | bytes 7077892
  730.0 6.6 copy-start.19
  730.0 8.4 %copy-start.1 = (bf16[768,2304]{1,0:T(8,128)(2,1)S(1)}, bf16[768,2304]{1,0:T(8,128)(2,1)}, u32[]{:S(2)}) copy-start(bf16[768,2304]{1,0:T(8,128)(2,1)} %param.17) | copy-start | bytes 10616836
  (48 other events, 111.5 us)
Sparse Core Ops, SparseCore 0:
  396.5 323.9 all-reduce.5
